TPU v7x, 32 devices: a whole 2x2x4 slice. The times are simulated.
32 devices in a mesh: row: 8 (over y, x, core), col: 4 (over z).
Axes of the slice: x: 2, y: 2, z: 4, core: 2. Of those that a mesh axis runs over, the one named last changes fastest.
Arguments:
- raw_rows: bfloat16 [32768, 64], P(('row', 'col')), may hold values from -6 to 6
- raw_wide: int32 [32768], P(('row', 'col')), may hold values from 0 to 1
- raw_dest: int32 [32768], P(('row', 'col')), may hold values from 0 to 31, as said below
- raw_slot: int32 [32768], P(('row', 'col')), may hold values from 0 to 511
- proj_narrow: bfloat16 [32, 128], replicated, may hold values from -1 to 1
- proj_wide: bfloat16 [64, 128], replicated, may hold values from -0.75 to 0.75
- adj_values: bfloat16 [8192, 8192], P('row', 'col'), may hold values from -1 to 1
- tile_mask: int32 [64, 64], P('row', 'col'), may hold values 0 or 1
- tile_scale: float32 [64, 64], P('row', 'col'), may hold values from 0.008286407 to 0.082864076
- weight_sum: bfloat16 [2, 128, 128], replicated, may hold values from -0.5 to 0.5
- weight_product: bfloat16 [2, 128, 128], replicated, may hold values from -0.5 to 0.5
Outputs:
- user_out: bfloat16 [8192, 128], P(('row', 'col'))
- item_out: bfloat16 [4, 2048, 128], P('col', 'row')
Inputs may be any that keep to these rules, and one draw needn't show every extreme that they name: `raw_dest`: among the feature rows stored on one device at most 96 have any one destination; one device, drawn from the seed, is the destination of exactly 96 rows of every device.
All inputs are finite; a program needn't handle non-finite values. No bound on the sum of `tile_mask` on one device may be relied on, other than what follows from the above.
Results may differ from a plain program's by a relative error of at most 0.025.
Values may be sent and summed in bfloat16 or wider, within the bound.
No kernel may reach another device: no remote copies, remote signals or barrier semaphores. Data moves between devices by JAX's collectives and lax.ppermute only.
A program may use at most 128 MiB of HBM per device.

v0:
```python
import functools

import jax
import jax.numpy as jnp
from jax import lax
from jax.experimental import pallas as pl
from jax.experimental.pallas import tpu as pltpu
from jax.sharding import PartitionSpec as P


TILE = 128
LANES = 128
CODE_ROWS = 8
F32 = jnp.float32
BF16 = jnp.bfloat16
NT = (((1,), (1,)), ((), ()))


def power_of_two(n):
    return n & (n - 1) == 0


def peer_to(i, k, n):
    return i ^ k if power_of_two(n) else (i + k) % n


def peer_from(i, k, n):
    return i ^ k if power_of_two(n) else (i + n - k) % n


def vmem_spec():
    return pl.BlockSpec(memory_space=pltpu.VMEM)


def params():
    return pltpu.CompilerParams(vmem_limit_bytes=24 * 2**20)


def whole_vmem():
    return pltpu.CompilerParams(vmem_limit_bytes=67_043_328)


def no_room():
    return pltpu.CompilerParams(vmem_limit_bytes=52 * 2**20)


def dispatch_kernel(devices, slots, *refs):
    sources, out_ref, (raw_ref, dest_ref, slot_ref, wide_ref), sems = (
        refs[:4],
        refs[4],
        refs[5:9],
        refs[9],
    )
    copies = [
        pltpu.make_async_copy(source, ref, sems.at[n])
        for n, (source, ref) in enumerate(
            zip(sources, (raw_ref, dest_ref, slot_ref, wide_ref), strict=True)
        )
    ]
    for copy in copies:
        copy.start()
    copies[1].wait()
    features, rows = raw_ref.shape
    chunks = rows // LANES
    dest = dest_ref[...]
    hot = (lax.broadcasted_iota(jnp.int32, (devices, rows), 0) == dest).astype(F32)
    hot_bf = hot.astype(BF16)
    before = lax.broadcasted_iota(jnp.int32, (LANES, 2 * LANES), 0)
    column = lax.broadcasted_iota(jnp.int32, (LANES, 2 * LANES), 1)
    prefix = ((before < column) | (column >= LANES)).astype(F32).astype(BF16)
    base = jnp.zeros((devices, LANES), F32)
    ranks = []
    for chunk in range(chunks):
        lanes = slice(chunk * LANES, (chunk + 1) * LANES)
        counted = jnp.dot(hot_bf[:, lanes], prefix, preferred_element_type=F32)
        ranks.append(
            jnp.sum((counted[:, :LANES] + base) * hot[:, lanes], axis=0, keepdims=True)
        )
        base = base + counted[:, LANES:]
    rank = jnp.concatenate(ranks, axis=1)
    place = (
        lax.broadcasted_iota(jnp.int32, (slots, rows), 0).astype(F32) == rank
    ).astype(F32).astype(BF16)
    for copy in (copies[0], copies[2], copies[3]):
        copy.wait()
    slot = slot_ref[...]
    code = lax.broadcasted_iota(jnp.int32, (2 * CODE_ROWS, rows), 0)
    codes = jnp.where(
        code == 0,
        slot // 256,
        jnp.where(code == 1, slot % 256, jnp.where(code == 2, wide_ref[...], 0)),
    )
    ext = jnp.concatenate([raw_ref[...], codes.astype(F32).astype(BF16)], axis=0)
    group = 8
    for first in range(0, devices, group):
        masked = jnp.concatenate(
            [ext * hot_bf[d : d + 1, :] for d in range(first, first + group)], axis=0
        )
        placed = lax.dot_general(masked, place, NT, preferred_element_type=F32).astype(BF16)
        for d in range(group):
            start = d * (features + 2 * CODE_ROWS)
            out_ref[first + d] = placed[start : start + features + CODE_ROWS]


def dispatch(raw, dest, slot, wide, devices, slots):
    features, rows = raw.shape
    return pl.pallas_call(
        functools.partial(dispatch_kernel, devices, slots),
        out_shape=jax.ShapeDtypeStruct((devices, features + CODE_ROWS, slots), BF16),
        in_specs=[pl.BlockSpec(memory_space=pltpu.HBM)] * 4,
        out_specs=vmem_spec(),
        scratch_shapes=[
            pltpu.VMEM(raw.shape, raw.dtype),
            *[pltpu.VMEM((1, rows), jnp.int32) for _ in range(3)],
            pltpu.SemaphoreType.DMA((4,)),
        ],
        compiler_params=whole_vmem(),
        name="dispatch",
    )(raw, dest, slot, wide)


def segment_kernel(narrow, upd, recv_ref, proj_narrow_ref, proj_wide_ref, *out_refs):
    user_ref, user_t_ref, item_ref, items_ref = out_refs
    devices, height, slots = recv_ref.shape
    features = height - CODE_ROWS
    nodes = user_ref.shape[0] + item_ref.shape[0]
    group = 8
    total = jnp.zeros((nodes, features + narrow), F32)
    for first in range(0, devices, group):
        block = jnp.concatenate([recv_ref[first + p] for p in range(group)], axis=1)
        codes = block[features:].astype(F32)
        node = (codes[0:1] * 256 + codes[1:2]).astype(jnp.int32)
        wide = codes[2:3].astype(BF16)
        rows = block[:features]
        values = jnp.concatenate([rows * wide, rows[:narrow] * (1 - wide)], axis=0)
        hot = (
            lax.broadcasted_iota(jnp.int32, (nodes, group * slots), 0) == node
        ).astype(F32).astype(BF16)
        total = total + lax.dot_general(hot, values, NT, preferred_element_type=F32)
    weights = jnp.concatenate([proj_wide_ref[...], proj_narrow_ref[...]], axis=0)
    initial = jnp.zeros((nodes, weights.shape[1]), F32)
    rest = total
    for _ in range(3):
        part = rest.astype(BF16)
        initial = initial + jnp.dot(part, weights, preferred_element_type=F32)
        rest = rest - part.astype(F32)
    users = initial[:upd]
    items = initial[upd:].astype(BF16)
    user_ref[...] = users.astype(BF16)
    user_t_ref[...] = users.T.astype(BF16)
    item_ref[...] = items
    for r in range(items_ref.shape[0]):
        items_ref[r] = items


def segment(recv, proj_narrow, proj_wide, upd, ipd, rows):
    d = proj_wide.shape[1]
    return pl.pallas_call(
        functools.partial(segment_kernel, proj_narrow.shape[0], upd),
        out_shape=(
            jax.ShapeDtypeStruct((upd, d), BF16),
            jax.ShapeDtypeStruct((d, upd), BF16),
            jax.ShapeDtypeStruct((ipd, d), BF16),
            jax.ShapeDtypeStruct((rows, ipd, d), BF16),
        ),
        in_specs=[vmem_spec()] * 3,
        out_specs=(vmem_spec(),) * 4,
        compiler_params=params(),
        name="segment",
    )(recv, proj_narrow, proj_wide)


def dequantize_kernel(mask_ref, scale_ref, values_ref, out_ref):
    i = pl.program_id(0)
    for j in range(values_ref.shape[1] // TILE):
        lanes = slice(j * TILE, (j + 1) * TILE)
        factor = mask_ref[i, j].astype(F32) * scale_ref[i, j]
        out_ref[:, lanes] = (values_ref[:, lanes].astype(F32) * factor).astype(BF16)


def dequantize(values, mask, scale):
    m, n = values.shape
    smem = pl.BlockSpec(memory_space=pltpu.SMEM)
    spec = pl.BlockSpec((TILE, n), lambda i: (i, 0))
    return pl.pallas_call(
        dequantize_kernel,
        out_shape=jax.ShapeDtypeStruct((m, n), BF16),
        grid=(m // TILE,),
        in_specs=[smem, smem, spec],
        out_specs=spec,
        compiler_params=no_room(),
        cost_estimate=pl.CostEstimate(flops=m * n, bytes_accessed=4 * m * n, transcendentals=0),
        name="dequantize",
    )(mask, scale, values)


def fetch_blocks(source, held, sems, order):
    upd = held.shape[1]
    copies = []
    for k, block in enumerate(order):
        start = pl.multiple_of(block * upd, upd)
        copies.append(
            pltpu.make_async_copy(source.at[pl.ds(start, upd), :], held.at[k], sems.at[k])
        )
        copies[-1].start()
    return copies


def user_sum_kernel(place_ref, adj_ref, items_ref, *refs):
    out_refs, (held, sems) = refs[:-2], refs[-2:]
    cols = len(out_refs)
    copies = fetch_blocks(
        adj_ref, held, sems, [peer_to(place_ref[0], k, cols) for k in range(cols)]
    )
    items = items_ref[...]
    for k, out_ref in enumerate(out_refs):
        copies[k].wait()
        out_ref[...] = jnp.dot(held[k], items, preferred_element_type=F32).astype(BF16)


def user_sums(place, adjacency, items, cols):
    m, n = adjacency.shape
    d = items.shape[1]
    return pl.pallas_call(
        user_sum_kernel,
        out_shape=(jax.ShapeDtypeStruct((m // cols, d), BF16),) * cols,
        in_specs=[
            pl.BlockSpec(memory_space=pltpu.SMEM),
            pl.BlockSpec(memory_space=pltpu.HBM),
            vmem_spec(),
        ],
        out_specs=(vmem_spec(),) * cols,
        scratch_shapes=[
            pltpu.VMEM((cols, m // cols, n), BF16),
            pltpu.SemaphoreType.DMA((cols,)),
        ],
        compiler_params=no_room(),
        cost_estimate=pl.CostEstimate(
            flops=2 * m * n * d, bytes_accessed=2 * m * n, transcendentals=0
        ),
        name="user_sums",
    )(place, adjacency, items)


def item_sum_kernel(place_ref, adj_ref, *refs):
    users_refs, (out_ref, held, total, sems) = refs[:-4], refs[-4:]
    cols = len(users_refs)
    rows, _, ipd = out_ref.shape
    copies = fetch_blocks(
        adj_ref, held, sems, [peer_from(place_ref[0], k, cols) for k in range(cols)]
    )
    for k in range(cols):
        copies[k].wait()
        users = users_refs[k][...]
        for r in range(rows):
            lanes = slice(r * ipd, (r + 1) * ipd)
            part = jnp.dot(users, held[k, :, lanes], preferred_element_type=F32)
            if k > 0:
                part = part + total[r]
            if k < cols - 1:
                total[r] = part
            else:
                out_ref[r] = part.astype(BF16)


def item_sums(place, adjacency, users_t, rows):
    m, n = adjacency.shape
    cols = len(users_t)
    d, _ = users_t[0].shape
    return pl.pallas_call(
        item_sum_kernel,
        out_shape=jax.ShapeDtypeStruct((rows, d, n // rows), BF16),
        in_specs=[
            pl.BlockSpec(memory_space=pltpu.SMEM),
            pl.BlockSpec(memory_space=pltpu.HBM),
        ]
        + [vmem_spec()] * cols,
        out_specs=vmem_spec(),
        scratch_shapes=[
            pltpu.VMEM((cols, m // cols, n), BF16),
            pltpu.VMEM((rows, d, n // rows), F32),
            pltpu.SemaphoreType.DMA((cols,)),
        ],
        compiler_params=no_room(),
        cost_estimate=pl.CostEstimate(
            flops=2 * m * n * d, bytes_accessed=2 * m * n, transcendentals=0
        ),
        name="item_sums",
    )(place, adjacency, *users_t)


def updated(side, own, weight_sum, weight_product):
    own = own.astype(F32)
    linear = jnp.dot((side + own).astype(BF16), weight_sum, preferred_element_type=F32)
    linear = linear + jnp.dot(
        (side * own).astype(BF16), weight_product, preferred_element_type=F32
    )
    return jnp.where(linear > 0, linear, 0.2 * linear)


def user_update_kernel(layer, own_ref, sum_ref, product_ref, *refs):
    parts, outs = refs[:-2], refs[-2:]
    side = parts[0][...].astype(F32)
    for part in parts[1:]:
        side = side + part[...].astype(F32)
    new = updated(side, own_ref[...], sum_ref[layer], product_ref[layer])
    outs[0][...] = new.astype(BF16)
    outs[1][...] = new.T.astype(BF16)


def user_update(layer, parts, own, weight_sum, weight_product):
    upd, d = own.shape
    return pl.pallas_call(
        functools.partial(user_update_kernel, layer),
        out_shape=(jax.ShapeDtypeStruct((upd, d), BF16), jax.ShapeDtypeStruct((d, upd), BF16)),
        in_specs=[vmem_spec()] * (3 + len(parts)),
        out_specs=(vmem_spec(),) * 2,
        compiler_params=params(),
        name="user_update",
    )(own, weight_sum, weight_product, *parts)


def item_update_kernel(layer, own_ref, sum_ref, product_ref, parts_ref, new_ref, *wide_refs):
    side = parts_ref[0].astype(F32)
    for r in range(1, parts_ref.shape[0]):
        side = side + parts_ref[r].astype(F32)
    new = updated(side.T, own_ref[...], sum_ref[layer], product_ref[layer]).astype(BF16)
    new_ref[...] = new
    for wide_ref in wide_refs:
        for r in range(wide_ref.shape[0]):
            wide_ref[r] = new


def item_update(layer, parts, own, weight_sum, weight_product, last):
    ipd, d = own.shape
    rows = parts.shape[0]
    outs = [jax.ShapeDtypeStruct((ipd, d), BF16)]
    if not last:
        outs.append(jax.ShapeDtypeStruct((rows, ipd, d), BF16))
    return pl.pallas_call(
        functools.partial(item_update_kernel, layer),
        out_shape=outs,
        in_specs=[vmem_spec()] * 4,
        out_specs=[vmem_spec()] * len(outs),
        compiler_params=params(),
        name="item_update",
    )(own, weight_sum, weight_product, parts)


def exchange(blocks, axis, n):
    received = [blocks[0]]
    for k in range(1, n):
        pairs = [(i, peer_to(i, k, n)) for i in range(n)]
        received.append(lax.ppermute(blocks[k], axis, pairs))
    return received


def per_device(
    raw_rows,
    raw_wide,
    raw_dest,
    raw_slot,
    proj_narrow,
    proj_wide,
    adj_values,
    tile_mask,
    tile_scale,
    weight_sum,
    weight_product,
):
    rows = lax.axis_size("row")
    cols = lax.axis_size("col")
    devices = rows * cols
    count = raw_rows.shape[0]
    capacity = 3 * count // devices
    slots = -(-capacity // LANES) * LANES
    upd = adj_values.shape[0] // cols
    ipd = adj_values.shape[1] // rows
    layers = weight_sum.shape[0]
    place = lax.axis_index("col").astype(jnp.int32).reshape(1)
    send = dispatch(
        raw_rows.T,
        raw_dest.reshape(1, count),
        raw_slot.reshape(1, count),
        raw_wide.reshape(1, count),
        devices,
        slots,
    )
    recv = lax.all_to_all(send, ("row", "col"), split_axis=0, concat_axis=0, tiled=True)
    adjacency = dequantize(adj_values, tile_mask, tile_scale)
    users, users_t, items, items_wide = segment(
        recv, proj_narrow, proj_wide, upd, ipd, rows
    )
    for layer in range(layers):
        last = layer == layers - 1
        all_items = lax.all_to_all(
            items_wide, "row", split_axis=0, concat_axis=0, tiled=True
        )
        all_users_t = exchange([users_t] * cols, "col", cols)
        item_parts = item_sums(place, adjacency, all_users_t, rows)
        item_parts = lax.all_to_all(
            item_parts, "row", split_axis=0, concat_axis=0, tiled=True
        )
        user_parts = user_sums(
            place, adjacency, all_items.reshape(rows * ipd, -1), cols
        )
        user_parts = exchange(user_parts, "col", cols)
        items, *wide = item_update(
            layer, item_parts, items, weight_sum, weight_product, last
        )
        items_wide = None if last else wide[0]
        users, users_t = user_update(
            layer, user_parts, users, weight_sum, weight_product
        )
    return (users, items[None])


def solution(mesh):
    placed = (
        P(("row", "col"), None),
        P(("row", "col")),
        P(("row", "col")),
        P(("row", "col")),
        P(),
        P(),
        P("row", "col"),
        P("row", "col"),
        P("row", "col"),
        P(),
        P(),
    )
    return jax.shard_map(
        per_device,
        mesh=mesh,
        in_specs=placed,
        out_specs=(P(("row", "col"), None), P("col", "row", None)),
        check_vma=False,
    )
```

profile of v0, /device:TPU:0, one launch (start us, length us, event | category | flops | bytes accessed | tf_op | source)
XLA Modules:
  0.0 117.9 jit_solution(10006682685072000753)
XLA Ops:
  0.6 3.3 %dispatch.1 = bf16[32,72,128]{2,1,0:T(8,128)(2,1)} custom-call(bf16[64,1024]{1,0:T(8,128)(2,1)} %bitcast.10, s32[1,1024]{1,0:T(1,128)} %bitcast.12, s32[1,1024]{1,0:T(1,128)} %bitcast.13, s32[1,1024]{1,0:T(1,128)} %bitcast.14), custom_call_target="tpu_custom_call" | custom-call | tf_op jit(solution)/shard_map/dispatch/pallas_call | solution.py:107
  4.0 22.9 %all_to_all.25.recv_ref = bf16[32,72,128]{2,1,0:T(8,128)(2,1)S(1)} all-to-all(bf16[32,72,128]{2,1,0:T(8,128)(2,1)} %dispatch.1), channel_id=1, replica_groups=mesh['row'=8,'col'=4] {'row','col'}, dimensions={0} | all-to-all | bytes 1179648 | tf_op jit(solution)/shard_map/all_to_all | solution.py:389
  26.8 0.7 copy-done.2
  27.6 0.7 copy-done.3
  28.3 2.4 %segment.1 = (bf16[256,128]{1,0:T(8,128)(2,1)S(1)}, bf16[128,256]{1,0:T(8,128)(2,1)S(1)}, bf16[256,128]{1,0:T(8,128)(2,1)S(1)}, bf16[8,256,128]{2,1,0:T(8,128)(2,1)}) custom-call(bf16[32,72,128]{2,1,0:T(8,128)(2,1)S(1)} %all_to_all.25.recv_ref, bf16[32,128]{1,0:T(8,128)(2,1)S(1)} %copy-done.3, bf16[64,128]{1,0:T(8,128)(2,1)S(1)} %copy-done.2), custom_call_target="tpu_custom_call" | custom-call | tf_op jit(solution)/shard_map/segment/pallas_call | solution.py:158
  30.7 2.7 %collective-permute-start.3 = (bf16[128,256]{1,0:T(8,128)(2,1)S(1)}, bf16[128,256]{1,0:T(8,128)(2,1)S(1)}, u32[]{:S(2)}, u32[]{:S(2)}) collective-permute-start(bf16[128,256]{1,0:T(8,128)(2,1)S(1)} %get-tuple-element.27.refs_0_), channel_id=1, source_target_pairs={{0,1},{1,0},{2,3},{3,2},{4,5},{5,4},{6,7},{7,6},{8,9},{9,8},{10,11... | collective-permute-start | bytes 196616 | tf_op jit(solution)/shard_map/ppermute | solution.py:354
  33.4 0.9 collective-permute-start.4
  34.3 1.5 %collective-permute-start.5 = (bf16[128,256]{1,0:T(8,128)(2,1)S(1)}, bf16[128,256]{1,0:T(8,128)(2,1)S(1)}, u32[]{:S(2)}, u32[]{:S(2)}) collective-permute-start(bf16[128,256]{1,0:T(8,128)(2,1)S(1)} %get-tuple-element.27.refs_0_), channel_id=1, source_target_pairs={{0,3},{1,2},{2,1},{3,0},{4,7},{5,6},{6,5},{7,4},{8,11},{9,10},{10,... | collective-permute-start | bytes 196616 | tf_op jit(solution)/shard_map/ppermute | solution.py:354
  35.7 0.7 copy-done.4
  36.4 0.7 copy-done.5
  37.1 7.0 %dequantize.1.adj_ref = bf16[1024,2048]{1,0:T(8,128)(2,1)} custom-call(s32[8,16]{1,0:T(8,128)S(1)} %copy-done.4, f32[8,16]{1,0:T(8,128)S(1)} %copy-done.5, bf16[1024,2048]{1,0:T(8,128)(2,1)} %values_ref.1), custom_call_target="tpu_custom_call" | custom-call | flops 2097152 | bytes 8388608 | tf_op jit(solution)/shard_map/dequantize/pallas_call | solution.py:185
  44.1 0.0 collective-permute-done.3.refs_1_
  44.2 0.0 collective-permute-done.4.refs_2_
  44.2 0.0 collective-permute-done.5.refs_3_
  44.2 2.6 %item_sums.2 = bf16[8,128,256]{2,1,0:T(8,128)(2,1)S(1)} custom-call(s32[1]{0:T(128)} %bitcast.4.place_ref, bf16[1024,2048]{1,0:T(8,128)(2,1)} %dequantize.1.adj_ref, bf16[128,256]{1,0:T(8,128)(2,1)S(1)} %get-tuple-element.27.refs_0_, bf16[128,256]{1,0:T(8,128)(2,1)S(1)} %collective-permute-done.3.refs_1_, ...), custom_call_target="tpu_custom_call" | custom-call | flops 536870912 | bytes 4194304 | tf_op jit(solution)/shard_map/item_sums/pallas_call | solution.py:270
  46.7 12.4 %all_to_all.26.parts_ref = bf16[8,128,256]{2,1,0:T(8,128)(2,1)S(1)} all-to-all(bf16[8,128,256]{2,1,0:T(8,128)(2,1)S(1)} %item_sums.2), channel_id=1, replica_groups=mesh['row'=8,'col'=4] {'row'}, dimensions={0} | all-to-all | bytes 1048576 | tf_op jit(solution)/shard_map/all_to_all | solution.py:401
  59.2 3.5 %all-to-all-start.1 = ((bf16[8,256,128]{2,1,0:T(8,128)(2,1)}), bf16[8,256,128]{2,1,0:T(8,128)(2,1)S(1)}, u32[]{:S(2)}, u32[]{:S(2)}) async-start(bf16[8,256,128]{2,1,0:T(8,128)(2,1)} %get-tuple-element.20), calls=%async_computation.1 | async-start | bytes 1048576 | tf_op jit(solution)/shard_map/all_to_all | solution.py:396
  62.7 0.0 copy-done
  62.7 1.1 item_update.2
  63.8 8.5 %all-to-all-done.1 = bf16[8,256,128]{2,1,0:T(8,128)(2,1)S(1)} async-done(((bf16[8,256,128]{2,1,0:T(8,128)(2,1)}), bf16[8,256,128]{2,1,0:T(8,128)(2,1)S(1)}, u32[]{:S(2)}, u32[]{:S(2)}) %all-to-all-start.1) | async-done | bytes 524320 | tf_op jit(solution)/shard_map/all_to_all | solution.py:396
  72.3 3.5 %all-to-all-start.3 = ((bf16[8,256,128]{2,1,0:T(8,128)(2,1)}), bf16[8,256,128]{2,1,0:T(8,128)(2,1)S(1)}, u32[]{:S(2)}, u32[]{:S(2)}) async-start(bf16[8,256,128]{2,1,0:T(8,128)(2,1)} %get-tuple-element.28), calls=%async_computation.3 | async-start | bytes 1048576 | tf_op jit(solution)/shard_map/all_to_all | solution.py:396
  75.8 3.0 %user_sums.2 = (bf16[256,128]{1,0:T(8,128)(2,1)S(1)}, bf16[256,128]{1,0:T(8,128)(2,1)S(1)}, bf16[256,128]{1,0:T(8,128)(2,1)S(1)}, bf16[256,128]{1,0:T(8,128)(2,1)S(1)}) custom-call(s32[1]{0:T(128)} %bitcast.4.place_ref, bf16[1024,2048]{1,0:T(8,128)(2,1)} %dequantize.1.adj_ref, bf16[2048,128]{1,0:T(8,128)(2,1)S(1)} %bitcast.9), custom_call_target="tpu_custom_call" | custom-call | flops 536870912 | bytes 4194304 | tf_op jit(solution)/shard_map/user_sums/pallas_call | solution.py:224
  78.8 0.9 collective-permute-start
  79.7 1.9 %collective-permute-start.1 = (bf16[256,128]{1,0:T(8,128)(2,1)S(1)}, bf16[256,128]{1,0:T(8,128)(2,1)S(1)}, u32[]{:S(2)}, u32[]{:S(2)}) collective-permute-start(bf16[256,128]{1,0:T(8,128)(2,1)S(1)} %get-tuple-element.23), channel_id=1, source_target_pairs={{0,2},{1,3},{2,0},{3,1},{4,6},{5,7},{6,4},{7,5},{8,10},{9,11},{10,... | collective-permute-start | bytes 196616 | tf_op jit(solution)/shard_map/ppermute | solution.py:354
  81.6 1.6 %collective-permute-start.2 = (bf16[256,128]{1,0:T(8,128)(2,1)S(1)}, bf16[256,128]{1,0:T(8,128)(2,1)S(1)}, u32[]{:S(2)}, u32[]{:S(2)}) collective-permute-start(bf16[256,128]{1,0:T(8,128)(2,1)S(1)} %get-tuple-element.24), channel_id=1, source_target_pairs={{0,3},{1,2},{2,1},{3,0},{4,7},{5,6},{6,5},{7,4},{8,11},{9,10},{10,... | collective-permute-start | bytes 196616 | tf_op jit(solution)/shard_map/ppermute | solution.py:354
  83.2 0.0 collective-permute-done.refs_1_
  83.2 5.0 %collective-permute-done.1.refs_2_ = bf16[256,128]{1,0:T(8,128)(2,1)S(1)} collective-permute-done((bf16[256,128]{1,0:T(8,128)(2,1)S(1)}, bf16[256,128]{1,0:T(8,128)(2,1)S(1)}, u32[]{:S(2)}, u32[]{:S(2)}) %collective-permute-start.1) | collective-permute-done | bytes 65568 | tf_op jit(solution)/shard_map/ppermute | solution.py:354
  88.2 0.0 collective-permute-done.2.refs_3_
  88.2 0.3 user_update.2
  88.5 1.3 %collective-permute-start.9 = (bf16[128,256]{1,0:T(8,128)(2,1)S(1)}, bf16[128,256]{1,0:T(8,128)(2,1)S(1)}, u32[]{:S(2)}, u32[]{:S(2)}) collective-permute-start(bf16[128,256]{1,0:T(8,128)(2,1)S(1)} %get-tuple-element.35.refs_0_), channel_id=1, source_target_pairs={{0,1},{1,0},{2,3},{3,2},{4,5},{5,4},{6,7},{7,6},{8,9},{9,8},{10,11... | collective-permute-start | bytes 196616 | tf_op jit(solution)/shard_map/ppermute | solution.py:354
  89.8 0.8 collective-permute-start.10
  90.6 2.3 %collective-permute-start.11 = (bf16[128,256]{1,0:T(8,128)(2,1)S(1)}, bf16[128,256]{1,0:T(8,128)(2,1)S(1)}, u32[]{:S(2)}, u32[]{:S(2)}) collective-permute-start(bf16[128,256]{1,0:T(8,128)(2,1)S(1)} %get-tuple-element.35.refs_0_), channel_id=1, source_target_pairs={{0,3},{1,2},{2,1},{3,0},{4,7},{5,6},{6,5},{7,4},{8,11},{9,10},{10,... | collective-permute-start | bytes 196616 | tf_op jit(solution)/shard_map/ppermute | solution.py:354
  92.9 0.3 collective-permute-done.9.refs_1_
  93.2 3.8 %collective-permute-done.10.refs_2_ = bf16[128,256]{1,0:T(8,128)(2,1)S(1)} collective-permute-done((bf16[128,256]{1,0:T(8,128)(2,1)S(1)}, bf16[128,256]{1,0:T(8,128)(2,1)S(1)}, u32[]{:S(2)}, u32[]{:S(2)}) %collective-permute-start.10) | collective-permute-done | bytes 65568 | tf_op jit(solution)/shard_map/ppermute | solution.py:354
  97.0 0.0 collective-permute-done.11.refs_3_
  97.0 3.3 %item_sums.3 = bf16[8,128,256]{2,1,0:T(8,128)(2,1)} custom-call(s32[1]{0:T(128)} %bitcast.4.place_ref, bf16[1024,2048]{1,0:T(8,128)(2,1)} %dequantize.1.adj_ref, bf16[128,256]{1,0:T(8,128)(2,1)S(1)} %get-tuple-element.35.refs_0_, bf16[128,256]{1,0:T(8,128)(2,1)S(1)} %collective-permute-done.9.refs_1_, bf16[128,256]{1,0:T(8,128)(2,1)S(1)} %collective-permute-done.10.refs_2_, ...), custom_call_target="tpu_custom_call" | custom-call | flops 536870912 | bytes 4194304 | tf_op jit(solution)/shard_map/item_sums/pallas_call | solution.py:270
  100.4 0.0 all-to-all-done.3
  100.4 3.9 %all-to-all-start.4 = ((bf16[8,128,256]{2,1,0:T(8,128)(2,1)}), bf16[8,128,256]{2,1,0:T(8,128)(2,1)S(1)}, u32[]{:S(2)}, u32[]{:S(2)}) async-start(bf16[8,128,256]{2,1,0:T(8,128)(2,1)} %item_sums.3), calls=%async_computation.4 | async-start | bytes 1048576 | tf_op jit(solution)/shard_map/all_to_all | solution.py:401
  104.2 2.9 %user_sums.3 = (bf16[256,128]{1,0:T(8,128)(2,1)S(1)}, bf16[256,128]{1,0:T(8,128)(2,1)S(1)}, bf16[256,128]{1,0:T(8,128)(2,1)S(1)}, bf16[256,128]{1,0:T(8,128)(2,1)S(1)}) custom-call(s32[1]{0:T(128)} %bitcast.4.place_ref, bf16[1024,2048]{1,0:T(8,128)(2,1)} %dequantize.1.adj_ref, bf16[2048,128]{1,0:T(8,128)(2,1)S(1)} %bitcast.8), custom_call_target="tpu_custom_call" | custom-call | flops 536870912 | bytes 4194304 | tf_op jit(solution)/shard_map/user_sums/pallas_call | solution.py:224
  107.2 1.3 %collective-permute-start.6 = (bf16[256,128]{1,0:T(8,128)(2,1)S(1)}, bf16[256,128]{1,0:T(8,128)(2,1)S(1)}, u32[]{:S(2)}, u32[]{:S(2)}) collective-permute-start(bf16[256,128]{1,0:T(8,128)(2,1)S(1)} %get-tuple-element.30), channel_id=1, source_target_pairs={{0,1},{1,0},{2,3},{3,2},{4,5},{5,4},{6,7},{7,6},{8,9},{9,8},{10,11... | collective-permute-start | bytes 196616 | tf_op jit(solution)/shard_map/ppermute | solution.py:354
  108.5 1.4 %collective-permute-start.7 = (bf16[256,128]{1,0:T(8,128)(2,1)S(1)}, bf16[256,128]{1,0:T(8,128)(2,1)S(1)}, u32[]{:S(2)}, u32[]{:S(2)}) collective-permute-start(bf16[256,128]{1,0:T(8,128)(2,1)S(1)} %get-tuple-element.31), channel_id=1, source_target_pairs={{0,2},{1,3},{2,0},{3,1},{4,6},{5,7},{6,4},{7,5},{8,10},{9,11},{10,... | collective-permute-start | bytes 196616 | tf_op jit(solution)/shard_map/ppermute | solution.py:354
  109.9 1.8 %collective-permute-start.8 = (bf16[256,128]{1,0:T(8,128)(2,1)S(1)}, bf16[256,128]{1,0:T(8,128)(2,1)S(1)}, u32[]{:S(2)}, u32[]{:S(2)}) collective-permute-start(bf16[256,128]{1,0:T(8,128)(2,1)S(1)} %get-tuple-element.32), channel_id=1, source_target_pairs={{0,3},{1,2},{2,1},{3,0},{4,7},{5,6},{6,5},{7,4},{8,11},{9,10},{10,... | collective-permute-start | bytes 196616 | tf_op jit(solution)/shard_map/ppermute | solution.py:354
  111.6 2.3 %all-to-all-done.4.parts_ref = bf16[8,128,256]{2,1,0:T(8,128)(2,1)S(1)} async-done(((bf16[8,128,256]{2,1,0:T(8,128)(2,1)}), bf16[8,128,256]{2,1,0:T(8,128)(2,1)S(1)}, u32[]{:S(2)}, u32[]{:S(2)}) %all-to-all-start.4) | async-done | bytes 524320 | tf_op jit(solution)/shard_map/all_to_all | solution.py:401
  114.0 0.9 item_update.3
  114.9 0.0 collective-permute-done.6.refs_1_
  114.9 2.1 %collective-permute-done.7.refs_2_ = bf16[256,128]{1,0:T(8,128)(2,1)S(1)} collective-permute-done((bf16[256,128]{1,0:T(8,128)(2,1)S(1)}, bf16[256,128]{1,0:T(8,128)(2,1)S(1)}, u32[]{:S(2)}, u32[]{:S(2)}) %collective-permute-start.7) | collective-permute-done | bytes 65568 | tf_op jit(solution)/shard_map/ppermute | solution.py:354
  117.0 0.0 collective-permute-done.8.refs_3_
  117.0 0.9 user_update.3
  (7 shorter events, 0.0 us)
Async XLA Ops:
  26.8 0.7 copy-start.2
  27.6 0.7 copy-start.3
  30.7 13.5 %collective-permute-start.3 = (bf16[128,256]{1,0:T(8,128)(2,1)S(1)}, bf16[128,256]{1,0:T(8,128)(2,1)S(1)}, u32[]{:S(2)}, u32[]{:S(2)}) collective-permute-start(bf16[128,256]{1,0:T(8,128)(2,1)S(1)} %get-tuple-element.27.refs_0_), channel_id=1, source_target_pairs={{0,1},{1,0},{2,3},{3,2},{4,5},{5,4},{6,7},{7,6},{8,9},{9,8},{10,11... | collective-permute-start | bytes 196616 | tf_op jit(solution)/shard_map/ppermute | solution.py:354
  33.4 10.8 %collective-permute-start.4 = (bf16[128,256]{1,0:T(8,128)(2,1)S(1)}, bf16[128,256]{1,0:T(8,128)(2,1)S(1)}, u32[]{:S(2)}, u32[]{:S(2)}) collective-permute-start(bf16[128,256]{1,0:T(8,128)(2,1)S(1)} %get-tuple-element.27.refs_0_), channel_id=1, source_target_pairs={{0,2},{1,3},{2,0},{3,1},{4,6},{5,7},{6,4},{7,5},{8,10},{9,11},{10,... | collective-permute-start | bytes 196616 | tf_op jit(solution)/shard_map/ppermute | solution.py:354
  34.3 9.9 %collective-permute-start.5 = (bf16[128,256]{1,0:T(8,128)(2,1)S(1)}, bf16[128,256]{1,0:T(8,128)(2,1)S(1)}, u32[]{:S(2)}, u32[]{:S(2)}) collective-permute-start(bf16[128,256]{1,0:T(8,128)(2,1)S(1)} %get-tuple-element.27.refs_0_), channel_id=1, source_target_pairs={{0,3},{1,2},{2,1},{3,0},{4,7},{5,6},{6,5},{7,4},{8,11},{9,10},{10,... | collective-permute-start | bytes 196616 | tf_op jit(solution)/shard_map/ppermute | solution.py:354
  35.7 0.7 copy-start.4
  36.4 0.7 copy-start.5
  44.1 18.5 %copy-start = (bf16[2,128,128]{2,1,0:T(8,128)(2,1)S(1)}, bf16[2,128,128]{2,1,0:T(8,128)(2,1)}, u32[]{:S(2)}) copy-start(bf16[2,128,128]{2,1,0:T(8,128)(2,1)} %sum_ref.7) | copy-start | bytes 196612
  44.1 18.5 %copy-start.1 = (bf16[2,128,128]{2,1,0:T(8,128)(2,1)S(1)}, bf16[2,128,128]{2,1,0:T(8,128)(2,1)}, u32[]{:S(2)}) copy-start(bf16[2,128,128]{2,1,0:T(8,128)(2,1)} %product_ref.7) | copy-start | bytes 196612
  59.2 13.1 %all-to-all-start.1 = ((bf16[8,256,128]{2,1,0:T(8,128)(2,1)}), bf16[8,256,128]{2,1,0:T(8,128)(2,1)S(1)}, u32[]{:S(2)}, u32[]{:S(2)}) async-start(bf16[8,256,128]{2,1,0:T(8,128)(2,1)} %get-tuple-element.20), calls=%async_computation.1 | async-start | bytes 1048576 | tf_op jit(solution)/shard_map/all_to_all | solution.py:396
  72.3 28.1 %all-to-all-start.3 = ((bf16[8,256,128]{2,1,0:T(8,128)(2,1)}), bf16[8,256,128]{2,1,0:T(8,128)(2,1)S(1)}, u32[]{:S(2)}, u32[]{:S(2)}) async-start(bf16[8,256,128]{2,1,0:T(8,128)(2,1)} %get-tuple-element.28), calls=%async_computation.3 | async-start | bytes 1048576 | tf_op jit(solution)/shard_map/all_to_all | solution.py:396
  78.8 4.5 %collective-permute-start = (bf16[256,128]{1,0:T(8,128)(2,1)S(1)}, bf16[256,128]{1,0:T(8,128)(2,1)S(1)}, u32[]{:S(2)}, u32[]{:S(2)}) collective-permute-start(bf16[256,128]{1,0:T(8,128)(2,1)S(1)} %get-tuple-element.22), channel_id=1, source_target_pairs={{0,1},{1,0},{2,3},{3,2},{4,5},{5,4},{6,7},{7,6},{8,9},{9,8},{10,11... | collective-permute-start | bytes 196616 | tf_op jit(solution)/shard_map/ppermute | solution.py:354
  79.7 8.5 %collective-permute-start.1 = (bf16[256,128]{1,0:T(8,128)(2,1)S(1)}, bf16[256,128]{1,0:T(8,128)(2,1)S(1)}, u32[]{:S(2)}, u32[]{:S(2)}) collective-permute-start(bf16[256,128]{1,0:T(8,128)(2,1)S(1)} %get-tuple-element.23), channel_id=1, source_target_pairs={{0,2},{1,3},{2,0},{3,1},{4,6},{5,7},{6,4},{7,5},{8,10},{9,11},{10,... | collective-permute-start | bytes 196616 | tf_op jit(solution)/shard_map/ppermute | solution.py:354
  81.6 6.6 %collective-permute-start.2 = (bf16[256,128]{1,0:T(8,128)(2,1)S(1)}, bf16[256,128]{1,0:T(8,128)(2,1)S(1)}, u32[]{:S(2)}, u32[]{:S(2)}) collective-permute-start(bf16[256,128]{1,0:T(8,128)(2,1)S(1)} %get-tuple-element.24), channel_id=1, source_target_pairs={{0,3},{1,2},{2,1},{3,0},{4,7},{5,6},{6,5},{7,4},{8,11},{9,10},{10,... | collective-permute-start | bytes 196616 | tf_op jit(solution)/shard_map/ppermute | solution.py:354
  88.5 4.8 %collective-permute-start.9 = (bf16[128,256]{1,0:T(8,128)(2,1)S(1)}, bf16[128,256]{1,0:T(8,128)(2,1)S(1)}, u32[]{:S(2)}, u32[]{:S(2)}) collective-permute-start(bf16[128,256]{1,0:T(8,128)(2,1)S(1)} %get-tuple-element.35.refs_0_), channel_id=1, source_target_pairs={{0,1},{1,0},{2,3},{3,2},{4,5},{5,4},{6,7},{7,6},{8,9},{9,8},{10,11... | collective-permute-start | bytes 196616 | tf_op jit(solution)/shard_map/ppermute | solution.py:354
  89.8 7.2 %collective-permute-start.10 = (bf16[128,256]{1,0:T(8,128)(2,1)S(1)}, bf16[128,256]{1,0:T(8,128)(2,1)S(1)}, u32[]{:S(2)}, u32[]{:S(2)}) collective-permute-start(bf16[128,256]{1,0:T(8,128)(2,1)S(1)} %get-tuple-element.35.refs_0_), channel_id=1, source_target_pairs={{0,2},{1,3},{2,0},{3,1},{4,6},{5,7},{6,4},{7,5},{8,10},{9,11},{10,... | collective-permute-start | bytes 196616 | tf_op jit(solution)/shard_map/ppermute | solution.py:354
  90.6 6.4 %collective-permute-start.11 = (bf16[128,256]{1,0:T(8,128)(2,1)S(1)}, bf16[128,256]{1,0:T(8,128)(2,1)S(1)}, u32[]{:S(2)}, u32[]{:S(2)}) collective-permute-start(bf16[128,256]{1,0:T(8,128)(2,1)S(1)} %get-tuple-element.35.refs_0_), channel_id=1, source_target_pairs={{0,3},{1,2},{2,1},{3,0},{4,7},{5,6},{6,5},{7,4},{8,11},{9,10},{10,... | collective-permute-start | bytes 196616 | tf_op jit(solution)/shard_map/ppermute | solution.py:354
  100.4 13.6 %all-to-all-start.4 = ((bf16[8,128,256]{2,1,0:T(8,128)(2,1)}), bf16[8,128,256]{2,1,0:T(8,128)(2,1)S(1)}, u32[]{:S(2)}, u32[]{:S(2)}) async-start(bf16[8,128,256]{2,1,0:T(8,128)(2,1)} %item_sums.3), calls=%async_computation.4 | async-start | bytes 1048576 | tf_op jit(solution)/shard_map/all_to_all | solution.py:401
  107.2 7.7 %collective-permute-start.6 = (bf16[256,128]{1,0:T(8,128)(2,1)S(1)}, bf16[256,128]{1,0:T(8,128)(2,1)S(1)}, u32[]{:S(2)}, u32[]{:S(2)}) collective-permute-start(bf16[256,128]{1,0:T(8,128)(2,1)S(1)} %get-tuple-element.30), channel_id=1, source_target_pairs={{0,1},{1,0},{2,3},{3,2},{4,5},{5,4},{6,7},{7,6},{8,9},{9,8},{10,11... | collective-permute-start | bytes 196616 | tf_op jit(solution)/shard_map/ppermute | solution.py:354
  108.5 8.5 %collective-permute-start.7 = (bf16[256,128]{1,0:T(8,128)(2,1)S(1)}, bf16[256,128]{1,0:T(8,128)(2,1)S(1)}, u32[]{:S(2)}, u32[]{:S(2)}) collective-permute-start(bf16[256,128]{1,0:T(8,128)(2,1)S(1)} %get-tuple-element.31), channel_id=1, source_target_pairs={{0,2},{1,3},{2,0},{3,1},{4,6},{5,7},{6,4},{7,5},{8,10},{9,11},{10,... | collective-permute-start | bytes 196616 | tf_op jit(solution)/shard_map/ppermute | solution.py:354
  109.9 7.1 %collective-permute-start.8 = (bf16[256,128]{1,0:T(8,128)(2,1)S(1)}, bf16[256,128]{1,0:T(8,128)(2,1)S(1)}, u32[]{:S(2)}, u32[]{:S(2)}) collective-permute-start(bf16[256,128]{1,0:T(8,128)(2,1)S(1)} %get-tuple-element.32), channel_id=1, source_target_pairs={{0,3},{1,2},{2,1},{3,0},{4,7},{5,6},{6,5},{7,4},{8,11},{9,10},{10,... | collective-permute-start | bytes 196616 | tf_op jit(solution)/shard_map/ppermute | solution.py:354
where the time goes:
time: 119 us; the launch traced here: 118 us
  blocking collectives  35.3 us (30%)
  starting transfers between devices  29.3 us (25%)
  Pallas kernels  27.7 us (23%)
  waiting for transfers between devices  22.1 us (19%)
  local copies, waits for them, and re-layouts  2.79 us (2%)
    all_to_all x1, blocking collectives, per_device(): lax.all_to_all(send, ('row', 'col'), split_axis=0, concat_axis=0, tiled=T...  22.9 us
    ppermute x12, starting transfers between devices, exchange(): received.append(lax.ppermute(blocks[k], axis, pairs))  18.4 us
    all_to_all x1, blocking collectives, per_device(): lax.all_to_all(item_parts, 'row', split_axis=0, concat_axis=0, tiled=True)  12.4 us
    ppermute x12, waiting for transfers between devices, exchange(): received.append(lax.ppermute(blocks[k], axis, pairs))  11.2 us
    all_to_all x2, waiting for transfers between devices, per_device(): lax.all_to_all(items_wide, 'row', split_axis=0, concat_axis=0, tiled=True)  8.54 us
    pallas_call x1, Pallas kernels, dequantize(): pl.pallas_call(dequantize_kernel, out_shape=jax.ShapeDtypeStruct((m, n),...  7.03 us
    all_to_all x2, starting transfers between devices, per_device(): lax.all_to_all(items_wide, 'row', split_axis=0, concat_axis=0, tiled=True)  6.98 us
    pallas_call x2, Pallas kernels, user_sums(): pl.pallas_call(user_sum_kernel, out_shape=(jax.ShapeDtypeStruct((m // col...  5.9 us
  transfers between devices with their start and end apart: 15, of which 6 were waited for; matrix products, arithmetic and copies ran while one was open for 0% of the time, Pallas kernels for 16%

commit v1 on v0

--- a/solution.py
+++ b/solution.py
@@ -22,10 +22,6 @@
 
 def peer_to(i, k, n):
     return i ^ k if power_of_two(n) else (i + k) % n
-
-
-def peer_from(i, k, n):
-    return i ^ k if power_of_two(n) else (i + n - k) % n
 
 
 def vmem_spec():
@@ -170,123 +166,102 @@
     )(recv, proj_narrow, proj_wide)
 
 
-def dequantize_kernel(mask_ref, scale_ref, values_ref, out_ref):
-    i = pl.program_id(0)
-    for j in range(values_ref.shape[1] // TILE):
-        lanes = slice(j * TILE, (j + 1) * TILE)
-        factor = mask_ref[i, j].astype(F32) * scale_ref[i, j]
-        out_ref[:, lanes] = (values_ref[:, lanes].astype(F32) * factor).astype(BF16)
-
-
-def dequantize(values, mask, scale):
+def dequantize_kernel(place_ref, mask_ref, scale_ref, values_ref, *refs):
+    out_refs, (held, sems) = refs[:-2], refs[-2:]
+    cols = len(out_refs)
+    upd, n = out_refs[0].shape
+    blocks = [peer_to(place_ref[0], k, cols) for k in range(cols)]
+    copies = []
+    for k, block in enumerate(blocks):
+        start = pl.multiple_of(block * upd, upd)
+        copies.append(
+            pltpu.make_async_copy(values_ref.at[pl.ds(start, upd), :], held.at[k], sems.at[k])
+        )
+        copies[-1].start()
+    for k, (block, out_ref) in enumerate(zip(blocks, out_refs, strict=True)):
+        copies[k].wait()
+        for i in range(upd // TILE):
+            row = block * (upd // TILE) + i
+            here = slice(i * TILE, (i + 1) * TILE)
+            for j in range(n // TILE):
+                lanes = slice(j * TILE, (j + 1) * TILE)
+                factor = mask_ref[row, j].astype(F32) * scale_ref[row, j]
+                out_ref[here, lanes] = (held[k, here, lanes].astype(F32) * factor).astype(BF16)
+
+
+def dequantize(place, values, mask, scale, cols):
     m, n = values.shape
     smem = pl.BlockSpec(memory_space=pltpu.SMEM)
-    spec = pl.BlockSpec((TILE, n), lambda i: (i, 0))
     return pl.pallas_call(
         dequantize_kernel,
-        out_shape=jax.ShapeDtypeStruct((m, n), BF16),
-        grid=(m // TILE,),
-        in_specs=[smem, smem, spec],
-        out_specs=spec,
-        compiler_params=no_room(),
-        cost_estimate=pl.CostEstimate(flops=m * n, bytes_accessed=4 * m * n, transcendentals=0),
-        name="dequantize",
-    )(mask, scale, values)
-
-
-def fetch_blocks(source, held, sems, order):
-    upd = held.shape[1]
-    copies = []
-    for k, block in enumerate(order):
-        start = pl.multiple_of(block * upd, upd)
-        copies.append(
-            pltpu.make_async_copy(source.at[pl.ds(start, upd), :], held.at[k], sems.at[k])
-        )
-        copies[-1].start()
-    return copies
-
-
-def user_sum_kernel(place_ref, adj_ref, items_ref, *refs):
-    out_refs, (held, sems) = refs[:-2], refs[-2:]
-    cols = len(out_refs)
-    copies = fetch_blocks(
-        adj_ref, held, sems, [peer_to(place_ref[0], k, cols) for k in range(cols)]
-    )
-    items = items_ref[...]
-    for k, out_ref in enumerate(out_refs):
-        copies[k].wait()
-        out_ref[...] = jnp.dot(held[k], items, preferred_element_type=F32).astype(BF16)
-
-
-def user_sums(place, adjacency, items, cols):
-    m, n = adjacency.shape
-    d = items.shape[1]
-    return pl.pallas_call(
-        user_sum_kernel,
-        out_shape=(jax.ShapeDtypeStruct((m // cols, d), BF16),) * cols,
-        in_specs=[
-            pl.BlockSpec(memory_space=pltpu.SMEM),
-            pl.BlockSpec(memory_space=pltpu.HBM),
-            vmem_spec(),
-        ],
+        out_shape=(jax.ShapeDtypeStruct((m // cols, n), BF16),) * cols,
+        in_specs=[smem, smem, smem, pl.BlockSpec(memory_space=pltpu.HBM)],
         out_specs=(vmem_spec(),) * cols,
         scratch_shapes=[
             pltpu.VMEM((cols, m // cols, n), BF16),
             pltpu.SemaphoreType.DMA((cols,)),
         ],
         compiler_params=no_room(),
+        cost_estimate=pl.CostEstimate(flops=m * n, bytes_accessed=4 * m * n, transcendentals=0),
+        name="dequantize",
+    )(place, mask, scale, values)
+
+
+def user_sum_kernel(cols, *refs):
+    adj_refs, items_ref, out_refs = refs[:cols], refs[cols], refs[cols + 1 :]
+    items = items_ref[...]
+    for adj_ref, out_ref in zip(adj_refs, out_refs, strict=True):
+        out_ref[...] = jnp.dot(adj_ref[...], items, preferred_element_type=F32).astype(BF16)
+
+
+def user_sums(adjacency, items):
+    cols = len(adjacency)
+    upd, n = adjacency[0].shape
+    d = items.shape[1]
+    return pl.pallas_call(
+        functools.partial(user_sum_kernel, cols),
+        out_shape=(jax.ShapeDtypeStruct((upd, d), BF16),) * cols,
+        in_specs=[vmem_spec()] * (cols + 1),
+        out_specs=(vmem_spec(),) * cols,
+        compiler_params=params(),
         cost_estimate=pl.CostEstimate(
-            flops=2 * m * n * d, bytes_accessed=2 * m * n, transcendentals=0
+            flops=2 * cols * upd * n * d, bytes_accessed=2 * cols * upd * n, transcendentals=0
         ),
         name="user_sums",
-    )(place, adjacency, items)
-
-
-def item_sum_kernel(place_ref, adj_ref, *refs):
-    users_refs, (out_ref, held, total, sems) = refs[:-4], refs[-4:]
-    cols = len(users_refs)
+    )(*adjacency, items)
+
+
+def item_sum_kernel(cols, *refs):
+    adj_refs, users_refs, out_ref = refs[:cols], refs[cols : 2 * cols], refs[-1]
     rows, _, ipd = out_ref.shape
-    copies = fetch_blocks(
-        adj_ref, held, sems, [peer_from(place_ref[0], k, cols) for k in range(cols)]
-    )
-    for k in range(cols):
-        copies[k].wait()
-        users = users_refs[k][...]
-        for r in range(rows):
-            lanes = slice(r * ipd, (r + 1) * ipd)
-            part = jnp.dot(users, held[k, :, lanes], preferred_element_type=F32)
-            if k > 0:
-                part = part + total[r]
-            if k < cols - 1:
-                total[r] = part
-            else:
-                out_ref[r] = part.astype(BF16)
-
-
-def item_sums(place, adjacency, users_t, rows):
-    m, n = adjacency.shape
-    cols = len(users_t)
-    d, _ = users_t[0].shape
-    return pl.pallas_call(
-        item_sum_kernel,
+    order = [0] + [k if power_of_two(cols) else cols - k for k in range(1, cols)]
+    users = [ref[...] for ref in users_refs]
+    for r in range(rows):
+        lanes = slice(r * ipd, (r + 1) * ipd)
+        total = None
+        for k in range(cols):
+            part = jnp.dot(
+                users[k], adj_refs[order[k]][:, lanes], preferred_element_type=F32
+            )
+            total = part if total is None else total + part
+        out_ref[r] = total.astype(BF16)
+
+
+def item_sums(adjacency, users_t, rows):
+    cols = len(adjacency)
+    upd, n = adjacency[0].shape
+    d = users_t[0].shape[0]
+    return pl.pallas_call(
+        functools.partial(item_sum_kernel, cols),
         out_shape=jax.ShapeDtypeStruct((rows, d, n // rows), BF16),
-        in_specs=[
-            pl.BlockSpec(memory_space=pltpu.SMEM),
-            pl.BlockSpec(memory_space=pltpu.HBM),
-        ]
-        + [vmem_spec()] * cols,
+        in_specs=[vmem_spec()] * (2 * cols),
         out_specs=vmem_spec(),
-        scratch_shapes=[
-            pltpu.VMEM((cols, m // cols, n), BF16),
-            pltpu.VMEM((rows, d, n // rows), F32),
-            pltpu.SemaphoreType.DMA((cols,)),
-        ],
-        compiler_params=no_room(),
+        compiler_params=params(),
         cost_estimate=pl.CostEstimate(
-            flops=2 * m * n * d, bytes_accessed=2 * m * n, transcendentals=0
+            flops=2 * cols * upd * n * d, bytes_accessed=2 * cols * upd * n, transcendentals=0
         ),
         name="item_sums",
-    )(place, adjacency, *users_t)
+    )(*adjacency, *users_t)
 
 
 def updated(side, own, weight_sum, weight_product):
@@ -387,27 +362,19 @@
         slots,
     )
     recv = lax.all_to_all(send, ("row", "col"), split_axis=0, concat_axis=0, tiled=True)
-    adjacency = dequantize(adj_values, tile_mask, tile_scale)
+    adjacency = dequantize(place, adj_values, tile_mask, tile_scale, cols)
     users, users_t, items, items_wide = segment(
         recv, proj_narrow, proj_wide, upd, ipd, rows
     )
     for layer in range(layers):
         last = layer == layers - 1
-        all_items = lax.all_to_all(
-            items_wide, "row", split_axis=0, concat_axis=0, tiled=True
-        )
+        all_items = lax.all_to_all(items_wide, "row", split_axis=0, concat_axis=0, tiled=True)
         all_users_t = exchange([users_t] * cols, "col", cols)
-        item_parts = item_sums(place, adjacency, all_users_t, rows)
-        item_parts = lax.all_to_all(
-            item_parts, "row", split_axis=0, concat_axis=0, tiled=True
-        )
-        user_parts = user_sums(
-            place, adjacency, all_items.reshape(rows * ipd, -1), cols
-        )
+        item_parts = item_sums(adjacency, all_users_t, rows)
+        item_parts = lax.all_to_all(item_parts, "row", split_axis=0, concat_axis=0, tiled=True)
+        user_parts = user_sums(adjacency, all_items.reshape(rows * ipd, -1))
         user_parts = exchange(user_parts, "col", cols)
-        items, *wide = item_update(
-            layer, item_parts, items, weight_sum, weight_product, last
-        )
+        items, *wide = item_update(layer, item_parts, items, weight_sum, weight_product, last)
         items_wide = None if last else wide[0]
         users, users_t = user_update(
             layer, user_parts, users, weight_sum, weight_product

time: 119 us -> 122 us (1.025)
  local copies, waits for them, and re-layouts: 2.79 us -> 14.4 us
  Pallas kernels: 27.7 us -> 19.7 us
  waiting for transfers between devices: 22.1 us -> 19.9 us
  starting transfers between devices: 29.3 us -> 30.8 us
    unnamed x12 -> x44, local copies, waits for them, and re-layouts: 2.79 us -> 14.4 us
    pallas_call x5, Pallas kernels: 18.8 us -> 11.3 us  [the longest x2 5.16 us: user_sums(): pl.pallas_call(functools.partial(user_sum_kernel, cols), out_shape=(jax.S...]
    all_to_all x2, waiting for transfers between devices: 8.54 us -> 6.74 us  [per_device(): lax.all_to_all(items_wide, 'row', split_axis=0, concat_axis=0, tiled=True)]
    all_to_all x2, starting transfers between devices: 6.98 us -> 8.29 us  [per_device(): lax.all_to_all(items_wide, 'row', split_axis=0, concat_axis=0, tiled=True)]
  transfers between devices with their start and end apart: 15 -> 15, of which waited for: 6 -> 5; matrix products, arithmetic and copies ran while one was open for 0% -> 0% of each run, Pallas kernels for 16% -> 11%
where the time goes in v1:
time: 122 us; the launch traced here: 121 us
  blocking collectives  35.7 us (29%)
  starting transfers between devices  30.8 us (25%)
  waiting for transfers between devices  19.9 us (16%)
  Pallas kernels  19.7 us (16%)
  local copies, waits for them, and re-layouts  14.4 us (12%)
    all_to_all x1, blocking collectives, per_device(): lax.all_to_all(send, ('row', 'col'), split_axis=0, concat_axis=0, tiled=T...  22.9 us
    ppermute x12, starting transfers between devices, exchange(): received.append(lax.ppermute(blocks[k], axis, pairs))  18.3 us
    unnamed x44, local copies, waits for them, and re-layouts  14.4 us
    all_to_all x1, blocking collectives, per_device(): lax.all_to_all(item_parts, 'row', split_axis=0, concat_axis=0, tiled=True)  12.8 us
    ppermute x12, waiting for transfers between devices, exchange(): received.append(lax.ppermute(blocks[k], axis, pairs))  11.9 us
    all_to_all x2, starting transfers between devices, per_device(): lax.all_to_all(items_wide, 'row', split_axis=0, concat_axis=0, tiled=True)  8.29 us
    all_to_all x2, waiting for transfers between devices, per_device(): lax.all_to_all(items_wide, 'row', split_axis=0, concat_axis=0, tiled=True)  6.74 us
    pallas_call x2, Pallas kernels, user_sums(): pl.pallas_call(functools.partial(user_sum_kernel, cols), out_shape=(jax.S...  5.16 us
  transfers between devices with their start and end apart: 15, of which 5 were waited for; matrix products, arithmetic and copies ran while one was open for 0% of the time, Pallas kernels for 11%

profile of v1, /device:TPU:0, one launch (start us, length us, event | category | flops | bytes accessed | tf_op | source)
XLA Modules:
  0.0 121.3 jit_solution(11627107780124494186)
XLA Ops:
  0.6 3.3 %dispatch.1 = bf16[32,72,128]{2,1,0:T(8,128)(2,1)} custom-call(bf16[64,1024]{1,0:T(8,128)(2,1)} %bitcast.8, s32[1,1024]{1,0:T(1,128)} %bitcast.10, s32[1,1024]{1,0:T(1,128)} %bitcast.11, s32[1,1024]{1,0:T(1,128)} %bitcast.12), custom_call_target="tpu_custom_call" | custom-call | tf_op jit(solution)/shard_map/dispatch/pallas_call | solution.py:103
  4.0 22.9 %all_to_all.25.recv_ref = bf16[32,72,128]{2,1,0:T(8,128)(2,1)S(1)} all-to-all(bf16[32,72,128]{2,1,0:T(8,128)(2,1)} %dispatch.1), channel_id=1, replica_groups=mesh['row'=8,'col'=4] {'row','col'}, dimensions={0} | all-to-all | bytes 1179648 | tf_op jit(solution)/shard_map/all_to_all | solution.py:364
  26.8 0.7 copy-done.18
  27.6 0.7 copy-done.19
  28.3 1.6 %segment.1 = (bf16[256,128]{1,0:T(8,128)(2,1)S(1)}, bf16[128,256]{1,0:T(8,128)(2,1)S(1)}, bf16[256,128]{1,0:T(8,128)(2,1)S(1)}, bf16[8,256,128]{2,1,0:T(8,128)(2,1)S(1)}) custom-call(bf16[32,72,128]{2,1,0:T(8,128)(2,1)S(1)} %all_to_all.25.recv_ref, bf16[32,128]{1,0:T(8,128)(2,1)S(1)} %copy-done.19, bf16[64,128]{1,0:T(8,128)(2,1)S(1)} %copy-done.18), custom_call_target="tpu_custom_call" | custom-call | tf_op jit(solution)/shard_map/segment/pallas_call | solution.py:154
  29.9 0.8 copy-done.13
  30.7 0.6 copy-done.14
  31.3 0.6 copy-done.16
  32.0 2.7 %collective-permute-start.3 = (bf16[128,256]{1,0:T(8,128)(2,1)S(1)}, bf16[128,256]{1,0:T(8,128)(2,1)S(1)}, u32[]{:S(2)}, u32[]{:S(2)}) collective-permute-start(bf16[128,256]{1,0:T(8,128)(2,1)S(1)} %get-tuple-element.35.refs_4_), channel_id=1, source_target_pairs={{0,1},{1,0},{2,3},{3,2},{4,5},{5,4},{6,7},{7,6},{8,9},{9,8},{10,11... | collective-permute-start | bytes 196616 | tf_op jit(solution)/shard_map/ppermute | solution.py:329
  34.6 0.9 collective-permute-start.4
  35.5 1.5 %collective-permute-start.5 = (bf16[128,256]{1,0:T(8,128)(2,1)S(1)}, bf16[128,256]{1,0:T(8,128)(2,1)S(1)}, u32[]{:S(2)}, u32[]{:S(2)}) collective-permute-start(bf16[128,256]{1,0:T(8,128)(2,1)S(1)} %get-tuple-element.35.refs_4_), channel_id=1, source_target_pairs={{0,3},{1,2},{2,1},{3,0},{4,7},{5,6},{6,5},{7,4},{8,11},{9,10},{10,... | collective-permute-start | bytes 196616 | tf_op jit(solution)/shard_map/ppermute | solution.py:329
  37.0 0.7 copy-done.20
  37.7 0.7 copy-done.21
  38.4 4.7 %dequantize.1 = (bf16[256,2048]{1,0:T(8,128)(2,1)S(1)}, bf16[256,2048]{1,0:T(8,128)(2,1)}, bf16[256,2048]{1,0:T(8,128)(2,1)}, bf16[256,2048]{1,0:T(8,128)(2,1)}) custom-call(s32[1]{0:T(128)} %bitcast.4.place_ref, s32[8,16]{1,0:T(8,128)S(1)} %copy-done.20, f32[8,16]{1,0:T(8,128)S(1)} %copy-done.21, bf16[1024,2048]{1,0:T(8,128)(2,1)} %values_ref.1), custom_call_target="tpu_custom_call" | custom-call | flops 2097152 | bytes 8388608 | tf_op jit(solution)/shard_map/dequantize/pallas_call | solution.py:195
  43.1 1.2 %copy-done = bf16[256,2048]{1,0:T(8,128)(2,1)S(1)} copy-done((bf16[256,2048]{1,0:T(8,128)(2,1)S(1)}, bf16[256,2048]{1,0:T(8,128)(2,1)}, u32[]{:S(2)}) %copy-start) | copy-done | bytes 1048600
  44.3 1.2 %copy-done.2 = bf16[256,2048]{1,0:T(8,128)(2,1)S(1)} copy-done((bf16[256,2048]{1,0:T(8,128)(2,1)S(1)}, bf16[256,2048]{1,0:T(8,128)(2,1)}, u32[]{:S(2)}) %copy-start.2) | copy-done | bytes 1048600
  45.6 1.2 %copy-done.4 = bf16[256,2048]{1,0:T(8,128)(2,1)S(1)} copy-done((bf16[256,2048]{1,0:T(8,128)(2,1)S(1)}, bf16[256,2048]{1,0:T(8,128)(2,1)}, u32[]{:S(2)}) %copy-start.4) | copy-done | bytes 1048600
  46.8 0.7 item_sums.2
  47.5 12.8 %all_to_all.26.parts_ref = bf16[8,128,256]{2,1,0:T(8,128)(2,1)} all-to-all(bf16[8,128,256]{2,1,0:T(8,128)(2,1)S(1)} %item_sums.2), channel_id=1, replica_groups=mesh['row'=8,'col'=4] {'row'}, dimensions={0} | all-to-all | bytes 1048576 | tf_op jit(solution)/shard_map/all_to_all | solution.py:374
  60.3 4.1 %all-to-all-start.1 = ((bf16[8,256,128]{2,1,0:T(8,128)(2,1)}), bf16[8,256,128]{2,1,0:T(8,128)(2,1)}, u32[]{:S(2)}, u32[]{:S(2)}) async-start(bf16[8,256,128]{2,1,0:T(8,128)(2,1)} %copy-done.13), calls=%async_computation.1 | async-start | bytes 1048576 | tf_op jit(solution)/shard_map/all_to_all | solution.py:371
  64.5 1.0 copy-done.9
  65.5 0.8 copy-done.17
  66.4 0.3 item_update.2
  66.7 0.8 copy-done.12
  67.5 6.7 %all-to-all-done.1 = bf16[8,256,128]{2,1,0:T(8,128)(2,1)} async-done(((bf16[8,256,128]{2,1,0:T(8,128)(2,1)}), bf16[8,256,128]{2,1,0:T(8,128)(2,1)}, u32[]{:S(2)}, u32[]{:S(2)}) %all-to-all-start.1) | async-done | bytes 524320 | tf_op jit(solution)/shard_map/all_to_all | solution.py:371
  74.2 4.1 %all-to-all-start.3 = ((bf16[8,256,128]{2,1,0:T(8,128)(2,1)}), bf16[8,256,128]{2,1,0:T(8,128)(2,1)}, u32[]{:S(2)}, u32[]{:S(2)}) async-start(bf16[8,256,128]{2,1,0:T(8,128)(2,1)} %copy-done.12), calls=%async_computation.3 | async-start | bytes 1048576 | tf_op jit(solution)/shard_map/all_to_all | solution.py:371
  78.4 1.2 %copy-done.5 = bf16[256,2048]{1,0:T(8,128)(2,1)S(1)} copy-done((bf16[256,2048]{1,0:T(8,128)(2,1)S(1)}, bf16[256,2048]{1,0:T(8,128)(2,1)}, u32[]{:S(2)}) %copy-start.5) | copy-done | bytes 1048600
  79.6 2.4 %user_sums.2 = (bf16[256,128]{1,0:T(8,128)(2,1)S(1)}, bf16[256,128]{1,0:T(8,128)(2,1)S(1)}, bf16[256,128]{1,0:T(8,128)(2,1)S(1)}, bf16[256,128]{1,0:T(8,128)(2,1)S(1)}) custom-call(bf16[256,2048]{1,0:T(8,128)(2,1)S(1)} %get-tuple-element.24.refs_0_, bf16[256,2048]{1,0:T(8,128)(2,1)S(1)} %copy-done.1, bf16[256,2048]{1,0:T(8,128)(2,1)S(1)} %copy-done.3, ...), custom_call_target="tpu_custom_call" | custom-call | flops 536870912 | bytes 4194304 | tf_op jit(solution)/shard_map/user_sums/pallas_call | solution.py:221
  82.0 1.2 collective-permute-start
  83.2 1.8 %collective-permute-start.1 = (bf16[256,128]{1,0:T(8,128)(2,1)S(1)}, bf16[256,128]{1,0:T(8,128)(2,1)S(1)}, u32[]{:S(2)}, u32[]{:S(2)}) collective-permute-start(bf16[256,128]{1,0:T(8,128)(2,1)S(1)} %get-tuple-element.31), channel_id=1, source_target_pairs={{0,2},{1,3},{2,0},{3,1},{4,6},{5,7},{6,4},{7,5},{8,10},{9,11},{10,... | collective-permute-start | bytes 196616 | tf_op jit(solution)/shard_map/ppermute | solution.py:329
  85.0 1.5 %collective-permute-start.2 = (bf16[256,128]{1,0:T(8,128)(2,1)S(1)}, bf16[256,128]{1,0:T(8,128)(2,1)S(1)}, u32[]{:S(2)}, u32[]{:S(2)}) collective-permute-start(bf16[256,128]{1,0:T(8,128)(2,1)S(1)} %get-tuple-element.32), channel_id=1, source_target_pairs={{0,3},{1,2},{2,1},{3,0},{4,7},{5,6},{6,5},{7,4},{8,11},{9,10},{10,... | collective-permute-start | bytes 196616 | tf_op jit(solution)/shard_map/ppermute | solution.py:329
  86.4 5.0 %collective-permute-done.1.refs_2_ = bf16[256,128]{1,0:T(8,128)(2,1)S(1)} collective-permute-done((bf16[256,128]{1,0:T(8,128)(2,1)S(1)}, bf16[256,128]{1,0:T(8,128)(2,1)S(1)}, u32[]{:S(2)}, u32[]{:S(2)}) %collective-permute-start.1) | collective-permute-done | bytes 65568 | tf_op jit(solution)/shard_map/ppermute | solution.py:329
  91.7 1.6 %collective-permute-start.9 = (bf16[128,256]{1,0:T(8,128)(2,1)S(1)}, bf16[128,256]{1,0:T(8,128)(2,1)S(1)}, u32[]{:S(2)}, u32[]{:S(2)}) collective-permute-start(bf16[128,256]{1,0:T(8,128)(2,1)S(1)} %get-tuple-element.43.refs_4_), channel_id=1, source_target_pairs={{0,1},{1,0},{2,3},{3,2},{4,5},{5,4},{6,7},{7,6},{8,9},{9,8},{10,11... | collective-permute-start | bytes 196616 | tf_op jit(solution)/shard_map/ppermute | solution.py:329
  93.3 0.6 collective-permute-start.10
  93.9 2.2 %collective-permute-start.11 = (bf16[128,256]{1,0:T(8,128)(2,1)S(1)}, bf16[128,256]{1,0:T(8,128)(2,1)S(1)}, u32[]{:S(2)}, u32[]{:S(2)}) collective-permute-start(bf16[128,256]{1,0:T(8,128)(2,1)S(1)} %get-tuple-element.43.refs_4_), channel_id=1, source_target_pairs={{0,3},{1,2},{2,1},{3,0},{4,7},{5,6},{6,5},{7,4},{8,11},{9,10},{10,... | collective-permute-start | bytes 196616 | tf_op jit(solution)/shard_map/ppermute | solution.py:329
  96.1 4.7 %collective-permute-done.10.refs_6_ = bf16[128,256]{1,0:T(8,128)(2,1)S(1)} collective-permute-done((bf16[128,256]{1,0:T(8,128)(2,1)S(1)}, bf16[128,256]{1,0:T(8,128)(2,1)S(1)}, u32[]{:S(2)}, u32[]{:S(2)}) %collective-permute-start.10) | collective-permute-done | bytes 65568 | tf_op jit(solution)/shard_map/ppermute | solution.py:329
  100.9 0.7 item_sums.3
  101.6 0.8 copy-done.8
  102.4 4.2 %all-to-all-start.4 = ((bf16[8,128,256]{2,1,0:T(8,128)(2,1)}), bf16[8,128,256]{2,1,0:T(8,128)(2,1)}, u32[]{:S(2)}, u32[]{:S(2)}) async-start(bf16[8,128,256]{2,1,0:T(8,128)(2,1)} %copy-done.8), calls=%async_computation.4 | async-start | bytes 1048576 | tf_op jit(solution)/shard_map/all_to_all | solution.py:374
  106.6 1.2 %copy-done.7 = bf16[256,2048]{1,0:T(8,128)(2,1)S(1)} copy-done((bf16[256,2048]{1,0:T(8,128)(2,1)S(1)}, bf16[256,2048]{1,0:T(8,128)(2,1)}, u32[]{:S(2)}) %copy-start.7) | copy-done | bytes 1048600
  107.8 2.8 %user_sums.3 = (bf16[256,128]{1,0:T(8,128)(2,1)S(1)}, bf16[256,128]{1,0:T(8,128)(2,1)}, bf16[256,128]{1,0:T(8,128)(2,1)}, bf16[256,128]{1,0:T(8,128)(2,1)S(1)}) custom-call(bf16[256,2048]{1,0:T(8,128)(2,1)S(1)} %get-tuple-element.24.refs_0_, bf16[256,2048]{1,0:T(8,128)(2,1)S(1)} %copy-done.1, bf16[256,2048]{1,0:T(8,128)(2,1)S(1)} %copy-done.3, ...), custom_call_target="tpu_custom_call" | custom-call | flops 536870912 | bytes 4194304 | tf_op jit(solution)/shard_map/user_sums/pallas_call | solution.py:221
  110.6 1.3 %collective-permute-start.6 = (bf16[256,128]{1,0:T(8,128)(2,1)}, bf16[256,128]{1,0:T(8,128)(2,1)S(1)}, u32[]{:S(2)}, u32[]{:S(2)}) collective-permute-start(bf16[256,128]{1,0:T(8,128)(2,1)} %get-tuple-element.38), channel_id=1, source_target_pairs={{0,1},{1,0},{2,3},{3,2},{4,5},{5,4},{6,7},{7,6},{8,9},{9,8},{10,11... | collective-permute-start | bytes 196616 | tf_op jit(solution)/shard_map/ppermute | solution.py:329
  111.9 1.2 collective-permute-start.7
  113.0 1.9 %collective-permute-start.8 = (bf16[256,128]{1,0:T(8,128)(2,1)S(1)}, bf16[256,128]{1,0:T(8,128)(2,1)S(1)}, u32[]{:S(2)}, u32[]{:S(2)}) collective-permute-start(bf16[256,128]{1,0:T(8,128)(2,1)S(1)} %get-tuple-element.40), channel_id=1, source_target_pairs={{0,3},{1,2},{2,1},{3,0},{4,7},{5,6},{6,5},{7,4},{8,11},{9,10},{10,... | collective-permute-start | bytes 196616 | tf_op jit(solution)/shard_map/ppermute | solution.py:329
  115.0 1.3 %all-to-all-done.4.parts_ref = bf16[8,128,256]{2,1,0:T(8,128)(2,1)} async-done(((bf16[8,128,256]{2,1,0:T(8,128)(2,1)}), bf16[8,128,256]{2,1,0:T(8,128)(2,1)}, u32[]{:S(2)}, u32[]{:S(2)}) %all-to-all-start.4) | async-done | bytes 524320 | tf_op jit(solution)/shard_map/all_to_all | solution.py:374
  116.3 1.9 %item_update.3 = bf16[256,128]{1,0:T(8,128)(2,1)} custom-call(bf16[256,128]{1,0:T(8,128)(2,1)S(1)} %get-tuple-element.42.own_ref, bf16[2,128,128]{2,1,0:T(8,128)(2,1)S(1)} %copy-done.10, bf16[2,128,128]{2,1,0:T(8,128)(2,1)S(1)} %copy-done.11, bf16[8,128,256]{2,1,0:T(8,128)(2,1)} %all-to-all-done.4.parts_ref), custom_call_target="tpu_custom_call" | custom-call | tf_op jit(solution)/shard_map/item_update/pallas_call | solution.py:315
  118.3 2.1 %collective-permute-done.7.refs_2_ = bf16[256,128]{1,0:T(8,128)(2,1)S(1)} collective-permute-done((bf16[256,128]{1,0:T(8,128)(2,1)}, bf16[256,128]{1,0:T(8,128)(2,1)S(1)}, u32[]{:S(2)}, u32[]{:S(2)}) %collective-permute-start.7) | collective-permute-done | bytes 65568 | tf_op jit(solution)/shard_map/ppermute | solution.py:329
  120.4 0.9 user_update.3
  (39 shorter events, 0.3 us)
Async XLA Ops:
  26.8 0.7 copy-start.18
  27.6 0.7 copy-start.19
  29.9 0.8 copy-start.13
  30.7 0.6 copy-start.14
  31.3 0.6 copy-start.16
  32.0 11.1 %collective-permute-start.3 = (bf16[128,256]{1,0:T(8,128)(2,1)S(1)}, bf16[128,256]{1,0:T(8,128)(2,1)S(1)}, u32[]{:S(2)}, u32[]{:S(2)}) collective-permute-start(bf16[128,256]{1,0:T(8,128)(2,1)S(1)} %get-tuple-element.35.refs_4_), channel_id=1, source_target_pairs={{0,1},{1,0},{2,3},{3,2},{4,5},{5,4},{6,7},{7,6},{8,9},{9,8},{10,11... | collective-permute-start | bytes 196616 | tf_op jit(solution)/shard_map/ppermute | solution.py:329
  34.6 8.4 %collective-permute-start.4 = (bf16[128,256]{1,0:T(8,128)(2,1)S(1)}, bf16[128,256]{1,0:T(8,128)(2,1)S(1)}, u32[]{:S(2)}, u32[]{:S(2)}) collective-permute-start(bf16[128,256]{1,0:T(8,128)(2,1)S(1)} %get-tuple-element.35.refs_4_), channel_id=1, source_target_pairs={{0,2},{1,3},{2,0},{3,1},{4,6},{5,7},{6,4},{7,5},{8,10},{9,11},{10,... | collective-permute-start | bytes 196616 | tf_op jit(solution)/shard_map/ppermute | solution.py:329
  35.5 7.6 %collective-permute-start.5 = (bf16[128,256]{1,0:T(8,128)(2,1)S(1)}, bf16[128,256]{1,0:T(8,128)(2,1)S(1)}, u32[]{:S(2)}, u32[]{:S(2)}) collective-permute-start(bf16[128,256]{1,0:T(8,128)(2,1)S(1)} %get-tuple-element.35.refs_4_), channel_id=1, source_target_pairs={{0,3},{1,2},{2,1},{3,0},{4,7},{5,6},{6,5},{7,4},{8,11},{9,10},{10,... | collective-permute-start | bytes 196616 | tf_op jit(solution)/shard_map/ppermute | solution.py:329
  37.0 0.7 copy-start.20
  37.7 0.7 copy-start.21
  38.4 26.1 %copy-start.10 = (bf16[2,128,128]{2,1,0:T(8,128)(2,1)S(1)}, bf16[2,128,128]{2,1,0:T(8,128)(2,1)}, u32[]{:S(2)}) copy-start(bf16[2,128,128]{2,1,0:T(8,128)(2,1)} %sum_ref.7) | copy-start | bytes 196612
  38.4 26.1 %copy-start.11 = (bf16[2,128,128]{2,1,0:T(8,128)(2,1)S(1)}, bf16[2,128,128]{2,1,0:T(8,128)(2,1)}, u32[]{:S(2)}) copy-start(bf16[2,128,128]{2,1,0:T(8,128)(2,1)} %product_ref.7) | copy-start | bytes 196612
  43.1 1.2 %copy-start = (bf16[256,2048]{1,0:T(8,128)(2,1)S(1)}, bf16[256,2048]{1,0:T(8,128)(2,1)}, u32[]{:S(2)}) copy-start(bf16[256,2048]{1,0:T(8,128)(2,1)} %get-tuple-element.25.refs_1_) | copy-start | bytes 3145732
  44.3 1.2 %copy-start.2 = (bf16[256,2048]{1,0:T(8,128)(2,1)S(1)}, bf16[256,2048]{1,0:T(8,128)(2,1)}, u32[]{:S(2)}) copy-start(bf16[256,2048]{1,0:T(8,128)(2,1)} %get-tuple-element.26.refs_2_) | copy-start | bytes 3145732
  45.6 1.2 %copy-start.4 = (bf16[256,2048]{1,0:T(8,128)(2,1)S(1)}, bf16[256,2048]{1,0:T(8,128)(2,1)}, u32[]{:S(2)}) copy-start(bf16[256,2048]{1,0:T(8,128)(2,1)} %get-tuple-element.27.refs_3_) | copy-start | bytes 3145732
  46.8 31.6 %copy-start.1 = (bf16[256,2048]{1,0:T(8,128)(2,1)S(1)}, bf16[256,2048]{1,0:T(8,128)(2,1)}, u32[]{:S(2)}) copy-start(bf16[256,2048]{1,0:T(8,128)(2,1)} %get-tuple-element.25.refs_1_) | copy-start | bytes 3145732
  46.8 31.6 %copy-start.3 = (bf16[256,2048]{1,0:T(8,128)(2,1)S(1)}, bf16[256,2048]{1,0:T(8,128)(2,1)}, u32[]{:S(2)}) copy-start(bf16[256,2048]{1,0:T(8,128)(2,1)} %get-tuple-element.26.refs_2_) | copy-start | bytes 3145732
  47.5 43.9 %copy-start.15 = (bf16[256,128]{1,0:T(8,128)(2,1)S(1)}, bf16[256,128]{1,0:T(8,128)(2,1)}, u32[]{:S(2)}) copy-start(bf16[256,128]{1,0:T(8,128)(2,1)} %copy-done.14) | copy-start | bytes 196612
  60.3 13.9 %all-to-all-start.1 = ((bf16[8,256,128]{2,1,0:T(8,128)(2,1)}), bf16[8,256,128]{2,1,0:T(8,128)(2,1)}, u32[]{:S(2)}, u32[]{:S(2)}) async-start(bf16[8,256,128]{2,1,0:T(8,128)(2,1)} %copy-done.13), calls=%async_computation.1 | async-start | bytes 1048576 | tf_op jit(solution)/shard_map/all_to_all | solution.py:371
  64.5 1.0 copy-start.9
  65.5 0.8 copy-start.17
  66.7 0.8 copy-start.12
  74.2 28.2 %all-to-all-start.3 = ((bf16[8,256,128]{2,1,0:T(8,128)(2,1)}), bf16[8,256,128]{2,1,0:T(8,128)(2,1)}, u32[]{:S(2)}, u32[]{:S(2)}) async-start(bf16[8,256,128]{2,1,0:T(8,128)(2,1)} %copy-done.12), calls=%async_computation.3 | async-start | bytes 1048576 | tf_op jit(solution)/shard_map/all_to_all | solution.py:371
  78.4 1.2 %copy-start.5 = (bf16[256,2048]{1,0:T(8,128)(2,1)S(1)}, bf16[256,2048]{1,0:T(8,128)(2,1)}, u32[]{:S(2)}) copy-start(bf16[256,2048]{1,0:T(8,128)(2,1)} %get-tuple-element.27.refs_3_) | copy-start | bytes 3145732
  79.6 21.3 %copy-start.6 = (bf16[256,2048]{1,0:T(8,128)(2,1)S(1)}, bf16[256,2048]{1,0:T(8,128)(2,1)}, u32[]{:S(2)}) copy-start(bf16[256,2048]{1,0:T(8,128)(2,1)} %get-tuple-element.27.refs_3_) | copy-start | bytes 3145732
  82.0 4.5 %collective-permute-start = (bf16[256,128]{1,0:T(8,128)(2,1)S(1)}, bf16[256,128]{1,0:T(8,128)(2,1)S(1)}, u32[]{:S(2)}, u32[]{:S(2)}) collective-permute-start(bf16[256,128]{1,0:T(8,128)(2,1)S(1)} %get-tuple-element.30), channel_id=1, source_target_pairs={{0,1},{1,0},{2,3},{3,2},{4,5},{5,4},{6,7},{7,6},{8,9},{9,8},{10,11... | collective-permute-start | bytes 196616 | tf_op jit(solution)/shard_map/ppermute | solution.py:329
  83.2 8.2 %collective-permute-start.1 = (bf16[256,128]{1,0:T(8,128)(2,1)S(1)}, bf16[256,128]{1,0:T(8,128)(2,1)S(1)}, u32[]{:S(2)}, u32[]{:S(2)}) collective-permute-start(bf16[256,128]{1,0:T(8,128)(2,1)S(1)} %get-tuple-element.31), channel_id=1, source_target_pairs={{0,2},{1,3},{2,0},{3,1},{4,6},{5,7},{6,4},{7,5},{8,10},{9,11},{10,... | collective-permute-start | bytes 196616 | tf_op jit(solution)/shard_map/ppermute | solution.py:329
  85.0 6.4 %collective-permute-start.2 = (bf16[256,128]{1,0:T(8,128)(2,1)S(1)}, bf16[256,128]{1,0:T(8,128)(2,1)S(1)}, u32[]{:S(2)}, u32[]{:S(2)}) collective-permute-start(bf16[256,128]{1,0:T(8,128)(2,1)S(1)} %get-tuple-element.32), channel_id=1, source_target_pairs={{0,3},{1,2},{2,1},{3,0},{4,7},{5,6},{6,5},{7,4},{8,11},{9,10},{10,... | collective-permute-start | bytes 196616 | tf_op jit(solution)/shard_map/ppermute | solution.py:329
  91.7 4.5 %collective-permute-start.9 = (bf16[128,256]{1,0:T(8,128)(2,1)S(1)}, bf16[128,256]{1,0:T(8,128)(2,1)S(1)}, u32[]{:S(2)}, u32[]{:S(2)}) collective-permute-start(bf16[128,256]{1,0:T(8,128)(2,1)S(1)} %get-tuple-element.43.refs_4_), channel_id=1, source_target_pairs={{0,1},{1,0},{2,3},{3,2},{4,5},{5,4},{6,7},{7,6},{8,9},{9,8},{10,11... | collective-permute-start | bytes 196616 | tf_op jit(solution)/shard_map/ppermute | solution.py:329
  93.3 7.6 %collective-permute-start.10 = (bf16[128,256]{1,0:T(8,128)(2,1)S(1)}, bf16[128,256]{1,0:T(8,128)(2,1)S(1)}, u32[]{:S(2)}, u32[]{:S(2)}) collective-permute-start(bf16[128,256]{1,0:T(8,128)(2,1)S(1)} %get-tuple-element.43.refs_4_), channel_id=1, source_target_pairs={{0,2},{1,3},{2,0},{3,1},{4,6},{5,7},{6,4},{7,5},{8,10},{9,11},{10,... | collective-permute-start | bytes 196616 | tf_op jit(solution)/shard_map/ppermute | solution.py:329
  93.9 7.0 %collective-permute-start.11 = (bf16[128,256]{1,0:T(8,128)(2,1)S(1)}, bf16[128,256]{1,0:T(8,128)(2,1)S(1)}, u32[]{:S(2)}, u32[]{:S(2)}) collective-permute-start(bf16[128,256]{1,0:T(8,128)(2,1)S(1)} %get-tuple-element.43.refs_4_), channel_id=1, source_target_pairs={{0,3},{1,2},{2,1},{3,0},{4,7},{5,6},{6,5},{7,4},{8,11},{9,10},{10,... | collective-permute-start | bytes 196616 | tf_op jit(solution)/shard_map/ppermute | solution.py:329
  101.6 0.8 copy-start.8
  102.4 13.9 %all-to-all-start.4 = ((bf16[8,128,256]{2,1,0:T(8,128)(2,1)}), bf16[8,128,256]{2,1,0:T(8,128)(2,1)}, u32[]{:S(2)}, u32[]{:S(2)}) async-start(bf16[8,128,256]{2,1,0:T(8,128)(2,1)} %copy-done.8), calls=%async_computation.4 | async-start | bytes 1048576 | tf_op jit(solution)/shard_map/all_to_all | solution.py:374
  106.6 1.2 %copy-start.7 = (bf16[256,2048]{1,0:T(8,128)(2,1)S(1)}, bf16[256,2048]{1,0:T(8,128)(2,1)}, u32[]{:S(2)}) copy-start(bf16[256,2048]{1,0:T(8,128)(2,1)} %get-tuple-element.27.refs_3_) | copy-start | bytes 3145732
  110.6 7.7 %collective-permute-start.6 = (bf16[256,128]{1,0:T(8,128)(2,1)}, bf16[256,128]{1,0:T(8,128)(2,1)S(1)}, u32[]{:S(2)}, u32[]{:S(2)}) collective-permute-start(bf16[256,128]{1,0:T(8,128)(2,1)} %get-tuple-element.38), channel_id=1, source_target_pairs={{0,1},{1,0},{2,3},{3,2},{4,5},{5,4},{6,7},{7,6},{8,9},{9,8},{10,11... | collective-permute-start | bytes 196616 | tf_op jit(solution)/shard_map/ppermute | solution.py:329
  111.9 8.5 %collective-permute-start.7 = (bf16[256,128]{1,0:T(8,128)(2,1)}, bf16[256,128]{1,0:T(8,128)(2,1)S(1)}, u32[]{:S(2)}, u32[]{:S(2)}) collective-permute-start(bf16[256,128]{1,0:T(8,128)(2,1)} %get-tuple-element.39), channel_id=1, source_target_pairs={{0,2},{1,3},{2,0},{3,1},{4,6},{5,7},{6,4},{7,5},{8,10},{9,11},{10,... | collective-permute-start | bytes 196616 | tf_op jit(solution)/shard_map/ppermute | solution.py:329
  113.0 7.4 %collective-permute-start.8 = (bf16[256,128]{1,0:T(8,128)(2,1)S(1)}, bf16[256,128]{1,0:T(8,128)(2,1)S(1)}, u32[]{:S(2)}, u32[]{:S(2)}) collective-permute-start(bf16[256,128]{1,0:T(8,128)(2,1)S(1)} %get-tuple-element.40), channel_id=1, source_target_pairs={{0,3},{1,2},{2,1},{3,0},{4,7},{5,6},{6,5},{7,4},{8,11},{9,10},{10,... | collective-permute-start | bytes 196616 | tf_op jit(solution)/shard_map/ppermute | solution.py:329
